TPU v7x, 32 devices: a whole 2x2x4 slice. The times are simulated.
32 devices in a mesh: grp: 2 (over y), kz: 4 (over z), coil: 2 (over x), kx: 2 (over core).
Axes of the slice: x: 2, y: 2, z: 4, core: 2. Of those that a mesh axis runs over, the one named last changes fastest.
Arguments:
- measured: float32 [2, 64, 32, 32, 32], P(None, ('grp', 'coil'), 'kx', 'kz'), parts along dimension 1, may hold values from -6 to 6
- mask: int32 [64, 32, 32], P(('grp', 'kx'), 'kz'), parts along dimension 0, may hold values 0 or 1
- kernel: float32 [27, 2, 32, 64], P(None, None, 'coil'), may hold values from -0.109375 to 0.109375
Outputs:
- restored: float32 [2, 64, 32, 32, 32], P(None, ('grp', 'coil'), 'kx', 'kz'), parts along dimension 1
There are 2 independent parts, one for each index of `grp`. A program takes and returns all parts, laid end to end along the dimension named above; an argument that names none is the same for every part. Nothing has to cross between parts.
All inputs are finite; a program needn't handle non-finite values. No bound on the sum of `mask` on one device may be relied on, other than what follows from the above.
Results may differ from a plain program's by a relative error of at most 0.0001.
Values sent between devices are 32-bit elements; how exact they have to be, the bound alone decides.
A program may use at most 128 MiB of HBM per device.

v0:
```python
import jax
import jax.numpy as jnp
from jax import lax
from jax.sharding import PartitionSpec as P

ITERS = 2


def partner(array, axis, apart):
    return lax.ppermute(array, axis, [(i, i ^ 1 << apart) for i in range(lax.axis_size(axis))])


def padded_2(array, sides, width):
    for axis, dim in sides:
        peers, length = (lax.axis_size(axis), array.shape[dim])
        up = [(i, (i + 1) % peers) for i in range(peers - 1)]
        down = [(j, i) for i, j in up]
        last = lax.slice_in_dim(array, length - width, length, axis=dim)
        first = lax.slice_in_dim(array, 0, width, axis=dim)
        before = lax.ppermute(last, axis, up)
        after = lax.ppermute(first, axis, down)
        array = jnp.concatenate([before, array, after], axis=dim)
    return array


def build_weights(kernel_part):
    real_k = kernel_part[:, 0]
    imag_k = kernel_part[:, 1]
    return jnp.concatenate(
        [jnp.concatenate([real_k, -imag_k], 2), jnp.concatenate([imag_k, real_k], 2)], 1
    )


def convolve(padded, weights, rows, depth, width):
    padded = jnp.pad(padded, ((0, 0), (0, 0), (0, 0), (0, 0), (1, 1)))
    shape = padded.shape
    line = width + 2
    plane = (depth + 2) * line
    extra = 2 * line + 2
    flat = padded.reshape(shape[0] * shape[1], -1)
    flat = jnp.pad(flat, ((0, 0), (0, extra)))
    out_rows = weights.shape[1]
    length = rows * plane
    result = jnp.zeros((out_rows, length), jnp.float32)
    for first in range(3):
        window = flat[:, first * plane : first * plane + length + extra]
        group = weights[9 * first : 9 * first + 9].reshape(9 * out_rows, -1)
        products = jnp.dot(group, window, precision=lax.Precision.HIGHEST)
        products = products.reshape(9, out_rows, length + extra)
        for second in range(3):
            for third in range(3):
                offset = third * line + second
                result = result + products[3 * second + third, :, offset : offset + length]
    result = result.reshape(2, out_rows // 2, rows, depth + 2, line)
    return result[:, :, :, :depth, :width]


def on_device(measured, mask, kernel):
    sampled = (mask == 1)[None, None]
    state = jnp.where(sampled, measured, jnp.zeros_like(measured))
    weights = build_weights(kernel)
    sign = jnp.array([1.0, -1.0], jnp.float32).reshape(2, 1, 1, 1, 1)
    kz_bits = lax.axis_size("kz").bit_length() - 1
    rows = measured.shape[2]
    depth = measured.shape[3]
    width = measured.shape[4]
    for step in range(ITERS):
        mirrored = state
        for bit in range(kz_bits):
            mirrored = partner(mirrored, "kz", bit)
        bit = 0
        mirrored = partner(mirrored, "kx", bit)
        own_virtual = jnp.flip(mirrored, (2, 3, 4)) * sign
        physical, virtual = (
            lax.all_gather(state, "coil", axis=1, tiled=True),
            lax.all_gather(own_virtual, "coil", axis=1, tiled=True),
        )
        stacked = jnp.concatenate([physical, virtual], 1)
        padded = padded_2(stacked, (("kz", 3), ("kx", 2)), 1)
        result = convolve(padded, weights, rows, depth, width)
        state = jnp.where(sampled, measured, result)
    return state


def solution(mesh):
    placed = (
        P(None, ("grp", "coil"), "kx", "kz", None),
        P(("grp", "kx"), "kz", None),
        P(None, None, "coil", None),
    )
    return jax.shard_map(
        on_device,
        mesh=mesh,
        in_specs=placed,
        out_specs=P(None, ("grp", "coil"), "kx", "kz", None),
        check_vma=False,
    )
```

profile of v0, /device:TPU:0, one launch (start us, length us, event | category | flops | bytes accessed | tf_op | source)
XLA Modules:
  0.0 728.0 jit_solution(10788578500702772405)
XLA Ops:
  12.3 45.7 %collective-permute-done = f32[2,16,16,8,32]{4,3,2,1,0:T(8,128)} collective-permute-done((f32[2,16,16,8,32]{4,3,2,1,0:T(8,128)S(1)}, f32[2,16,16,8,32]{4,3,2,1,0:T(8,128)}, u32[]{:S(2)}, u32[]{:S(2)}) %collective-permute-start) | collective-permute-done | bytes 524320 | tf_op jit(solution)/shard_map/ppermute | solution.py:10
  60.9 90.1 %collective-permute-done.1 = f32[2,16,16,8,32]{4,3,2,1,0:T(8,128)} collective-permute-done((f32[2,16,16,8,32]{4,3,2,1,0:T(8,128)}, f32[2,16,16,8,32]{4,3,2,1,0:T(8,128)}, u32[]{:S(2)}, u32[]{:S(2)}) %collective-permute-start.1) | collective-permute-done | bytes 524320 | tf_op jit(solution)/shard_map/ppermute | solution.py:10
  151.0 4.5 collective-permute-done.2
  160.0 4.7 constant_dynamic-update-slice_fusion.1
  164.7 53.1 %all-gather.7.cloned.1.call-done = f32[2,32,16,8,32]{4,3,2,1,0:T(8,128)} async-done(((f32[2,16,16,8,32]{4,3,2,1,0:T(8,128)}), f32[2,32,16,8,32]{4,3,2,1,0:T(8,128)}) %all-gather.7.cloned.1.call-update) | async-done | bytes 1048592 | tf_op jit(solution)/shard_map/all_gather | solution.py:76
  217.8 4.7 constant_dynamic-update-slice_fusion
  222.5 8.2 %fusion.16 = (f32[2,64,16,1,32]{4,3,2,1,0:T(1,128)S(1)}, f32[2,64,16,1,32]{4,3,2,1,0:T(1,128)S(1)}) fusion(f32[2,64,16,8,32]{4,3,2,1,0:T(8,128)} %constant_dynamic-update-slice_fusion), kind=kLoop, calls=%fused_computation.85 | loop fusion | bytes 1048576 | tf_op jit(solution)/shard_map/slice | solution.py:18
  231.3 3.4 collective-permute-start.3
  236.7 7.8 %copy.17 = f32[2,64,16,8,32]{1,4,3,2,0:T(8,128)} copy(f32[2,64,16,8,32]{4,3,2,1,0:T(8,128)} %constant_dynamic-update-slice_fusion) | data formatting | bytes 4194304 | tf_op jit(solution)/shard_map/concatenate | solution.py:78
  245.7 4.8 collective-permute-done.4
  257.1 8.4 %copy.25 = f32[2,64,18,10,32]{1,0,4,3,2:T(2,128)} copy(f32[2,64,18,10,32]{1,4,3,2,0:T(8,128)S(1)} %pad_maximum_fusion) | data formatting | bytes 5898240
  265.5 7.4 %pad.14.clone = f32[2,64,18,10,34]{1,0,4,3,2:T(2,128)} pad(f32[2,64,18,10,32]{1,0,4,3,2:T(2,128)} %copy.25, f32[]{:T(128)} %constant.2.clone.1), padding=0_0x0_0x0_0x0_0x1_1 | pad | bytes 6082564 | tf_op jit(solution)/shard_map/jit(_pad)/pad | solution.py:35
  272.9 6.0 reshape.97
  279.0 6.2 fusion.8
  285.2 5.2 fusion.9
  290.4 7.6 %fusion.1 = f32[9,32,5510]{2,1,0:T(8,128)} fusion(f32[27,32,128]{2,1,0:T(8,128)S(1)} %copy-done.7, f32[128,6120]{0,1:T(8,128)S(1)} %reshape.97), kind=kOutput, calls=%fused_computation.7 | convolution fusion | flops 2437447680 | bytes 9923328 | tf_op jit(solution)/shard_map/dot_general | solution.py:48
  304.3 3.4 squeeze.162
  307.7 5.9 fusion.20
  313.6 4.3 squeeze.163
  317.8 4.2 squeeze.164
  322.0 4.4 squeeze.165
  326.4 4.3 squeeze.166
  343.8 3.4 squeeze.171
  347.2 11.6 %add_add_fusion.1 = f32[2,16,16,10,34]{4,3,2,1,0:T(8,128)} fusion(f32[2,16,16,10,34]{4,3,2,1,0:T(8,128)} %squeeze.165, f32[2,16,16,10,34]{4,3,2,1,0:T(8,128)} %squeeze.164, f32[2,16,16,10,34]{4,3,2,1,0:T(8,128)} %squeeze.163, f32[2,16,16,10,34]{4,3,2,1,0:T(8,128)} %reshape.121, f32[2,16,16,10,34]{4,3,2,1,0:T(8,128)} %squeeze.162), kind=kLoop, calls=%fused_computation.3 | loop fusion | flops 696320 | bytes 4177920 | tf_op jit(solution)/shard_map/add | solution.py:53
  358.8 7.8 %fusion.11 = f32[2,16,16,8,32]{4,3,2,1,0:T(8,128)} fusion(f32[2,16,16,8,32]{4,3,2,1,0:T(8,128)S(1)} %copy-done.2, f32[2,16,16,10,34]{4,3,2,1,0:T(8,128)} %squeeze.171, f32[2,16,16,10,34]{4,3,2,1,0:T(8,128)} %squeeze.170, f32[2,16,16,10,34]{4,3,2,1,0:T(8,128)} %squeeze.169, f32[2,16,16,10,34]{4,3,2,1,0:T(8,128)} %squeeze.168, ...), kind=kLoop, calls=%fused_computation.26 | loop fusion | flops 917504 | bytes 4722688 | tf_op jit(solution)/shard_map/jit(_where)/select_n | solution.py:81
  368.0 46.5 %collective-permute-done.7 = f32[2,16,16,8,32]{4,3,2,1,0:T(8,128)} collective-permute-done((f32[2,16,16,8,32]{4,3,2,1,0:T(8,128)}, f32[2,16,16,8,32]{4,3,2,1,0:T(8,128)}, u32[]{:S(2)}, u32[]{:S(2)}) %collective-permute-start.7) | collective-permute-done | bytes 524320 | tf_op jit(solution)/shard_map/ppermute | solution.py:10
  417.0 90.4 %collective-permute-done.8 = f32[2,16,16,8,32]{4,3,2,1,0:T(8,128)S(1)} collective-permute-done((f32[2,16,16,8,32]{4,3,2,1,0:T(8,128)}, f32[2,16,16,8,32]{4,3,2,1,0:T(8,128)S(1)}, u32[]{:S(2)}, u32[]{:S(2)}) %collective-permute-start.8) | collective-permute-done | bytes 524320 | tf_op jit(solution)/shard_map/ppermute | solution.py:10
  507.4 4.3 collective-permute-done.9
  516.5 4.7 constant_dynamic-update-slice_fusion.3
  521.2 51.2 %all-gather.11.cloned.1.call-done = f32[2,32,16,8,32]{4,3,2,1,0:T(8,128)} async-done(((f32[2,16,16,8,32]{4,3,2,1,0:T(8,128)}), f32[2,32,16,8,32]{4,3,2,1,0:T(8,128)}) %all-gather.11.cloned.1.call-update) | async-done | bytes 1048592 | tf_op jit(solution)/shard_map/all_gather | solution.py:76
  572.4 4.8 constant_dynamic-update-slice_fusion.2
  577.2 8.3 %fusion.15 = (f32[2,64,16,1,32]{4,3,2,1,0:T(1,128)S(1)}, f32[2,64,16,1,32]{4,3,2,1,0:T(1,128)S(1)}) fusion(f32[2,64,16,8,32]{4,3,2,1,0:T(8,128)} %constant_dynamic-update-slice_fusion.2), kind=kLoop, calls=%fused_computation.84 | loop fusion | bytes 1048576 | tf_op jit(solution)/shard_map/slice | solution.py:18
  586.1 3.4 collective-permute-start.10
  591.4 7.9 %copy.21 = f32[2,64,16,8,32]{1,4,3,2,0:T(8,128)} copy(f32[2,64,16,8,32]{4,3,2,1,0:T(8,128)} %constant_dynamic-update-slice_fusion.2) | data formatting | bytes 4194304 | tf_op jit(solution)/shard_map/concatenate | solution.py:78
  600.5 4.8 collective-permute-done.11
  611.9 8.4 %copy.26 = f32[2,64,18,10,32]{1,0,4,3,2:T(2,128)} copy(f32[2,64,18,10,32]{1,4,3,2,0:T(8,128)S(1)} %pad_maximum_fusion.1) | data formatting | bytes 5898240
  620.3 7.4 %pad.16.clone = f32[2,64,18,10,34]{1,0,4,3,2:T(2,128)} pad(f32[2,64,18,10,32]{1,0,4,3,2:T(2,128)} %copy.26, f32[]{:T(128)} %constant.2.clone.1), padding=0_0x0_0x0_0x0_0x1_1 | pad | bytes 6082564 | tf_op jit(solution)/shard_map/jit(_pad)/pad | solution.py:35
  627.7 6.0 reshape.98
  633.7 6.2 fusion.6
  640.0 5.2 fusion.7
  645.2 7.3 %fusion.4 = f32[9,32,5510]{2,1,0:T(8,128)} fusion(f32[27,32,128]{2,1,0:T(8,128)S(1)} %copy-done.8, f32[128,6120]{0,1:T(8,128)S(1)} %reshape.98), kind=kOutput, calls=%fused_computation.9 | convolution fusion | flops 2437447680 | bytes 9923328 | tf_op jit(solution)/shard_map/dot_general | solution.py:48
  662.1 5.9 fusion.18
  668.0 4.2 squeeze.185
  672.3 4.2 squeeze.186
  676.5 4.5 squeeze.187
  680.9 4.3 squeeze.188
  701.7 11.6 %add_add_fusion = f32[2,16,16,10,34]{4,3,2,1,0:T(8,128)} fusion(f32[2,16,16,10,34]{4,3,2,1,0:T(8,128)} %squeeze.187, f32[2,16,16,10,34]{4,3,2,1,0:T(8,128)} %squeeze.186, f32[2,16,16,10,34]{4,3,2,1,0:T(8,128)} %squeeze.185, f32[2,16,16,10,34]{4,3,2,1,0:T(8,128)} %reshape.122, f32[2,16,16,10,34]{4,3,2,1,0:T(8,128)} %squeeze.184), kind=kLoop, calls=%fused_computation.2 | loop fusion | flops 696320 | bytes 4177920 | tf_op jit(solution)/shard_map/add | solution.py:53
  713.3 7.8 %fusion.10 = f32[2,16,16,8,32]{4,3,2,1,0:T(8,128)} fusion(f32[2,16,16,8,32]{4,3,2,1,0:T(8,128)S(1)} %copy-done.3, f32[2,16,16,10,34]{4,3,2,1,0:T(8,128)} %squeeze.193, f32[2,16,16,10,34]{4,3,2,1,0:T(8,128)} %squeeze.192, f32[2,16,16,10,34]{4,3,2,1,0:T(8,128)} %squeeze.191, f32[2,16,16,10,34]{4,3,2,1,0:T(8,128)} %squeeze.190, ...), kind=kLoop, calls=%fused_computation.19 | loop fusion | flops 917504 | bytes 4722688 | tf_op jit(solution)/shard_map/jit(_where)/select_n | solution.py:81
  (81 shorter events, 87.8 us)
Async XLA Ops:
  6.5 153.5 %all-gather.5.cloned.1.call-start = ((), (), s32[]{:S(2)}) async-start(), calls=%async_computation | async-start | bytes 6291456 | tf_op jit(solution)/shard_map/all_gather | solution.py:75
  9.1 51.6 %copy-start.6 = (f32[2,16,16,8,32]{4,3,2,1,0:T(8,128)}, f32[2,16,16,8,32]{4,3,2,1,0:T(8,128)S(1)}, u32[]{:S(2)}) copy-start(f32[2,16,16,8,32]{4,3,2,1,0:T(8,128)S(1)} %broadcast_select_fusion) | copy-start | bytes 1572868
  9.2 149.1 %copy-start.10 = (f32[2]{0:T(128)S(1)}, f32[2]{0:T(128)}, u32[]{:S(2)}) copy-start(f32[2]{0:T(128)} %constant.8.clone) | copy-start | bytes 28
  9.2 48.9 %collective-permute-start = (f32[2,16,16,8,32]{4,3,2,1,0:T(8,128)S(1)}, f32[2,16,16,8,32]{4,3,2,1,0:T(8,128)}, u32[]{:S(2)}, u32[]{:S(2)}) collective-permute-start(f32[2,16,16,8,32]{4,3,2,1,0:T(8,128)S(1)} %broadcast_select_fusion), channel_id=1, source_target_pairs={{0,4},{4,0},{8,12},{12,8},{1,5},{5,1},{9,13},{13,9},{2,6},{6,2},{1... | collective-permute-start | bytes 1572872 | tf_op jit(solution)/shard_map/ppermute | solution.py:10
  58.0 93.0 %collective-permute-start.1 = (f32[2,16,16,8,32]{4,3,2,1,0:T(8,128)}, f32[2,16,16,8,32]{4,3,2,1,0:T(8,128)}, u32[]{:S(2)}, u32[]{:S(2)}) collective-permute-start(f32[2,16,16,8,32]{4,3,2,1,0:T(8,128)} %collective-permute-done), channel_id=1, source_target_pairs={{0,8},{4,12},{8,0},{12,4},{1,9},{5,13},{9,1},{13,5},{2,10},{6,14},... | collective-permute-start | bytes 1572872 | tf_op jit(solution)/shard_map/ppermute | solution.py:10
  60.8 157.0 %all-gather.7.cloned.1.call-start = ((), (), s32[]{:S(2)}) async-start(), calls=%async_computation.1 | async-start | bytes 6291456 | tf_op jit(solution)/shard_map/all_gather | solution.py:76
  151.0 4.5 collective-permute-start.2
  159.9 356.6 %all-gather.9.cloned.1.call-start = ((), (), s32[]{:S(2)}) async-start(), calls=%async_computation.2 | async-start | bytes 6291456 | tf_op jit(solution)/shard_map/all_gather | solution.py:75
  222.5 14.1 %copy-start.9 = (f32[27,2,16,64]{3,2,1,0:T(8,128)S(1)}, f32[27,2,16,64]{3,2,1,0:T(8,128)}, u32[]{:S(2)}) copy-start(f32[27,2,16,64]{3,2,1,0:T(8,128)} %param.6) | copy-start | bytes 663556
  231.3 14.4 %collective-permute-start.3 = (f32[2,64,16,1,32]{1,4,3,2,0:T(8,128)S(1)}, f32[2,64,16,1,32]{1,4,3,2,0:T(8,128)S(1)}, u32[]{:S(2)}, u32[]{:S(2)}) collective-permute-start(f32[2,64,16,1,32]{1,4,3,2,0:T(8,128)S(1)} %copy.15), channel_id=1, source_target_pairs={{0,4},{4,8},{8,12},{1,5},{5,9},{9,13},{2,6},{6,10},{10,14},{3,7},{... | collective-permute-start | bytes 786440 | tf_op jit(solution)/shard_map/ppermute | solution.py:20
  235.3 15.1 %collective-permute-start.4 = (f32[2,64,16,1,32]{1,4,3,2,0:T(8,128)S(1)}, f32[2,64,16,1,32]{1,4,3,2,0:T(8,128)S(1)}, u32[]{:S(2)}, u32[]{:S(2)}) collective-permute-start(f32[2,64,16,1,32]{1,4,3,2,0:T(8,128)S(1)} %copy.16), channel_id=1, source_target_pairs={{4,0},{8,4},{12,8},{5,1},{9,5},{13,9},{6,2},{10,6},{14,10},{7,3},{... | collective-permute-start | bytes 786440 | tf_op jit(solution)/shard_map/ppermute | solution.py:21
  244.5 11.9 %copy-start = (f32[2,64,16,8,32]{1,4,3,2,0:T(8,128)S(1)}, f32[2,64,16,8,32]{1,4,3,2,0:T(8,128)}, u32[]{:S(2)}) copy-start(f32[2,64,16,8,32]{1,4,3,2,0:T(8,128)} %copy.17) | copy-start | bytes 6291460
  251.6 3.8 collective-permute-start.5
  252.9 3.5 collective-permute-start.6
  279.0 6.2 copy-start.7
  347.2 11.6 %copy-start.2 = (f32[2,16,16,8,32]{4,3,2,1,0:T(8,128)S(1)}, f32[2,16,16,8,32]{4,3,2,1,0:T(8,128)}, u32[]{:S(2)}) copy-start(f32[2,16,16,8,32]{4,3,2,1,0:T(8,128)} %param.4) | copy-start | bytes 1572868
  347.2 11.6 %copy-start.5 = (f32[2,16,16,10,34]{4,3,2,1,0:T(8,128)S(1)}, f32[2,16,16,10,34]{4,3,2,1,0:T(8,128)}, u32[]{:S(2)}) copy-start(f32[2,16,16,10,34]{4,3,2,1,0:T(8,128)} %squeeze.166) | copy-start | bytes 2088964
  366.5 48.0 %collective-permute-start.7 = (f32[2,16,16,8,32]{4,3,2,1,0:T(8,128)}, f32[2,16,16,8,32]{4,3,2,1,0:T(8,128)}, u32[]{:S(2)}, u32[]{:S(2)}) collective-permute-start(f32[2,16,16,8,32]{4,3,2,1,0:T(8,128)} %fusion.11), channel_id=1, source_target_pairs={{0,4},{4,0},{8,12},{12,8},{1,5},{5,1},{9,13},{13,9},{2,6},{6,2},{1... | collective-permute-start | bytes 1572872 | tf_op jit(solution)/shard_map/ppermute | solution.py:10
  414.5 92.9 %collective-permute-start.8 = (f32[2,16,16,8,32]{4,3,2,1,0:T(8,128)}, f32[2,16,16,8,32]{4,3,2,1,0:T(8,128)S(1)}, u32[]{:S(2)}, u32[]{:S(2)}) collective-permute-start(f32[2,16,16,8,32]{4,3,2,1,0:T(8,128)} %collective-permute-done.7), channel_id=1, source_target_pairs={{0,8},{4,12},{8,0},{12,4},{1,9},{5,13},{9,1},{13,5},{2,10},{6,14},... | collective-permute-start | bytes 1572872 | tf_op jit(solution)/shard_map/ppermute | solution.py:10
  416.9 155.5 %all-gather.11.cloned.1.call-start = ((), (), s32[]{:S(2)}) async-start(), calls=%async_computation.3 | async-start | bytes 6291456 | tf_op jit(solution)/shard_map/all_gather | solution.py:76
  507.4 4.3 collective-permute-start.9
  586.1 14.4 %collective-permute-start.10 = (f32[2,64,16,1,32]{1,4,3,2,0:T(8,128)S(1)}, f32[2,64,16,1,32]{1,4,3,2,0:T(8,128)S(1)}, u32[]{:S(2)}, u32[]{:S(2)}) collective-permute-start(f32[2,64,16,1,32]{1,4,3,2,0:T(8,128)S(1)} %copy.19), channel_id=1, source_target_pairs={{0,4},{4,8},{8,12},{1,5},{5,9},{9,13},{2,6},{6,10},{10,14},{3,7},{... | collective-permute-start | bytes 786440 | tf_op jit(solution)/shard_map/ppermute | solution.py:20
  590.1 15.1 %collective-permute-start.11 = (f32[2,64,16,1,32]{1,4,3,2,0:T(8,128)S(1)}, f32[2,64,16,1,32]{1,4,3,2,0:T(8,128)S(1)}, u32[]{:S(2)}, u32[]{:S(2)}) collective-permute-start(f32[2,64,16,1,32]{1,4,3,2,0:T(8,128)S(1)} %copy.20), channel_id=1, source_target_pairs={{4,0},{8,4},{12,8},{5,1},{9,5},{13,9},{6,2},{10,6},{14,10},{7,3},{... | collective-permute-start | bytes 786440 | tf_op jit(solution)/shard_map/ppermute | solution.py:21
  599.3 11.9 %copy-start.1 = (f32[2,64,16,8,32]{1,4,3,2,0:T(8,128)S(1)}, f32[2,64,16,8,32]{1,4,3,2,0:T(8,128)}, u32[]{:S(2)}) copy-start(f32[2,64,16,8,32]{1,4,3,2,0:T(8,128)} %copy.21) | copy-start | bytes 6291460
  606.3 2.6 collective-permute-start.12
  607.7 3.5 collective-permute-start.13
  633.7 6.2 copy-start.8
  701.7 11.6 %copy-start.3 = (f32[2,16,16,8,32]{4,3,2,1,0:T(8,128)S(1)}, f32[2,16,16,8,32]{4,3,2,1,0:T(8,128)}, u32[]{:S(2)}) copy-start(f32[2,16,16,8,32]{4,3,2,1,0:T(8,128)} %param.4) | copy-start | bytes 1572868
  701.7 11.6 %copy-start.4 = (f32[2,16,16,10,34]{4,3,2,1,0:T(8,128)S(1)}, f32[2,16,16,10,34]{4,3,2,1,0:T(8,128)}, u32[]{:S(2)}) copy-start(f32[2,16,16,10,34]{4,3,2,1,0:T(8,128)} %squeeze.188) | copy-start | bytes 2088964
Sparse Core Ops, SparseCore 0:
  60.9 55.9 all-gather.4
  160.1 57.7 all-gather.6
  417.0 54.8 all-gather.8
  516.6 55.7 all-gather.10
where the time goes:
time: 734 us; the launch traced here: 728 us
  waiting for transfers between devices  401 us (55%)
  local copies, waits for them, and re-layouts  195 us (27%)
  other arithmetic  55.1 us (8%)
  matrix products  37.7 us (5%)
  starting transfers between devices  24.6 us (3%)
  between operations  13.9 us (2%)
    ppermute x6, waiting for transfers between devices, partner(): lax.ppermute(array, axis, [(i, i ^ 1 << apart) for i in range(lax.axis_si...  282 us
    all_gather x2, waiting for transfers between devices, on_device(): lax.all_gather(own_virtual, 'coil', axis=1, tiled=True)  104 us
    squeeze x20, local copies, waits for them, and re-layouts, convolve(): result = result + products[3 * second + third, :, offset:offset + length]  73.9 us
    dot_general x6, matrix products, convolve(): products = jnp.dot(group, window, precision=lax.Precision.HIGHEST)  37.7 us
    unnamed x26, local copies, waits for them, and re-layouts  26.3 us
    concatenate x4, local copies, waits for them, and re-layouts, on_device(): stacked = jnp.concatenate([physical, virtual], 1)  25.1 us
    add x2, other arithmetic, convolve(): result = result + products[3 * second + third, :, offset:offset + length]  23.2 us
    slice x4, local copies, waits for them, and re-layouts, padded_2(): last = lax.slice_in_dim(array, length - width, length, axis=dim)  17.7 us
  transfers between devices with their start and end apart: 18, of which 14 were waited for; matrix products, arithmetic and copies ran while one was open for 5% of the time, Pallas kernels for 0%

commit v1 on v0

--- a/solution.py
+++ b/solution.py
@@ -4,6 +4,18 @@
 from jax.sharding import PartitionSpec as P
 
 ITERS = 2
+
+
+def collect(x, axis, dim):
+    ways, here = (lax.axis_size(axis), lax.axis_index(axis))
+    grown, reach = (x, 1)
+    while reach < ways:
+        theirs = lax.ppermute(grown, axis, [(d, d ^ reach) for d in range(ways)])
+        mine_first = jnp.concatenate([grown, theirs], axis=dim)
+        theirs_first = jnp.concatenate([theirs, grown], axis=dim)
+        grown = jnp.where(here & reach == 0, mine_first, theirs_first)
+        reach = 2 * reach
+    return grown
 
 
 def partner(array, axis, apart):
@@ -73,7 +85,7 @@
         own_virtual = jnp.flip(mirrored, (2, 3, 4)) * sign
         physical, virtual = (
             lax.all_gather(state, "coil", axis=1, tiled=True),
-            lax.all_gather(own_virtual, "coil", axis=1, tiled=True),
+            collect(own_virtual, "coil", 1),
         )
         stacked = jnp.concatenate([physical, virtual], 1)
         padded = padded_2(stacked, (("kz", 3), ("kx", 2)), 1)

time: 734 us -> 806 us (1.098)
  waiting for transfers between devices: 401 us -> 465 us
  other arithmetic: 55.1 us -> 94.6 us
  local copies, waits for them, and re-layouts: 195 us -> 160 us
    ppermute x0 -> x2, waiting for transfers between devices: none -> 180 us  [collect(): theirs = lax.ppermute(grown, axis, [(d, d ^ reach) for d in range(ways)])]
    all_gather x2 -> x0, waiting for transfers between devices: 104 us -> none  [on_device(): lax.all_gather(own_virtual, 'coil', axis=1, tiled=True)]
    concatenate x0 -> x4, other arithmetic: none -> 33 us  [on_device(): stacked = jnp.concatenate([physical, virtual], 1)]
    slice x4 -> x2, local copies, waits for them, and re-layouts: 17.7 us -> 1.19 us  [padded_2(): last = lax.slice_in_dim(array, length - width, length, axis=dim)]
    ppermute x4, waiting for transfers between devices: 12.8 us -> 3 us  [padded_2(): after = lax.ppermute(first, axis, down)]
    concatenate x4 -> x2, local copies, waits for them, and re-layouts: 25.1 us -> 15.6 us  [on_device(): stacked = jnp.concatenate([physical, virtual], 1)]
    unnamed x26 -> x24, local copies, waits for them, and re-layouts: 26.3 us -> 16.9 us
  transfers between devices with their start and end apart: 18 -> 18, of which waited for: 14 -> 10; matrix products, arithmetic and copies ran while one was open for 5% -> 6% of each run, Pallas kernels for 0% -> 0%
where the time goes in v1:
time: 806 us; the launch traced here: 799 us
  waiting for transfers between devices  465 us (58%)
  local copies, waits for them, and re-layouts  160 us (20%)
  other arithmetic  94.6 us (12%)
  matrix products  37.7 us (5%)
  starting transfers between devices  28.5 us (4%)
  between operations  13.9 us (2%)
    ppermute x6, waiting for transfers between devices, partner(): lax.ppermute(array, axis, [(i, i ^ 1 << apart) for i in range(lax.axis_si...  281 us
    ppermute x2, waiting for transfers between devices, collect(): theirs = lax.ppermute(grown, axis, [(d, d ^ reach) for d in range(ways)])  180 us
    squeeze x20, local copies, waits for them, and re-layouts, convolve(): result = result + products[3 * second + third, :, offset:offset + length]  74.1 us
    dot_general x6, matrix products, convolve(): products = jnp.dot(group, window, precision=lax.Precision.HIGHEST)  37.7 us
    concatenate x4, other arithmetic, on_device(): stacked = jnp.concatenate([physical, virtual], 1)  33 us
    add x2, other arithmetic, convolve(): result = result + products[3 * second + third, :, offset:offset + length]  23.2 us
    unnamed x24, local copies, waits for them, and re-layouts  16.9 us
  transfers between devices with their start and end apart: 18, of which 10 were waited for; matrix products, arithmetic and copies ran while one was open for 6% of the time, Pallas kernels for 0%

profile of v1, /device:TPU:0, one launch (start us, length us, event | category | flops | bytes accessed | tf_op | source)
XLA Modules:
  0.0 799.3 jit_solution(6404079393465468620)
XLA Ops:
  12.3 45.6 %collective-permute-done = f32[2,16,16,8,32]{4,3,2,1,0:T(8,128)S(1)} collective-permute-done((f32[2,16,16,8,32]{4,3,2,1,0:T(8,128)S(1)}, f32[2,16,16,8,32]{4,3,2,1,0:T(8,128)S(1)}, u32[]{:S(2)}, u32[]{:S(2)}) %collective-permute-start) | collective-permute-done | bytes 524320 | tf_op jit(solution)/shard_map/ppermute | solution.py:22
  60.7 90.0 %collective-permute-done.1 = f32[2,16,16,8,32]{4,3,2,1,0:T(8,128)} collective-permute-done((f32[2,16,16,8,32]{4,3,2,1,0:T(8,128)S(1)}, f32[2,16,16,8,32]{4,3,2,1,0:T(8,128)}, u32[]{:S(2)}, u32[]{:S(2)}) %collective-permute-start.1) | collective-permute-done | bytes 524320 | tf_op jit(solution)/shard_map/ppermute | solution.py:22
  150.8 4.4 collective-permute-done.2
  161.0 91.2 %collective-permute-done.3 = f32[2,16,16,8,32]{4,3,2,1,0:T(8,128)S(1)} collective-permute-done((f32[2,16,16,8,32]{4,3,2,1,0:T(8,128)}, f32[2,16,16,8,32]{4,3,2,1,0:T(8,128)S(1)}, u32[]{:S(2)}, u32[]{:S(2)}) %collective-permute-start.3) | collective-permute-done | bytes 524320 | tf_op jit(solution)/shard_map/ppermute | solution.py:13
  252.2 5.0 maximum_select_fusion
  257.2 8.3 %fusion.14 = (f32[2,64,16,1,32]{4,3,2,1,0:T(1,128)S(1)}, f32[2,64,16,1,32]{4,3,2,1,0:T(1,128)S(1)}) fusion(f32[2,32,16,8,32]{4,3,2,1,0:T(8,128)} %all-gather.3.cloned.1.call-done, f32[2,32,16,8,32]{4,3,2,1,0:T(8,128)} %maximum_select_fusion), kind=kLoop, calls=%fused_computation.46 | loop fusion | flops 131072 | bytes 2621440 | tf_op jit(solution)/shard_map/concatenate | solution.py:90
  269.5 8.4 %pad_maximum_fusion = f32[2,64,16,8,32]{4,3,2,1,0:T(8,128)} fusion(f32[2,32,16,8,32]{4,3,2,1,0:T(8,128)} %maximum_select_fusion, f32[2,32,16,8,32]{4,3,2,1,0:T(8,128)} %all-gather.3.cloned.1.call-done), kind=kLoop, calls=%fused_computation.2 | loop fusion | flops 524288 | bytes 4194304 | tf_op jit(solution)/shard_map/concatenate | solution.py:90
  277.8 7.8 copy.17
  292.6 8.4 %copy.25 = f32[2,64,18,10,32]{1,0,4,3,2:T(2,128)} copy(f32[2,64,18,10,32]{1,4,3,2,0:T(8,128)S(1)} %pad_maximum_fusion.2) | data formatting | bytes 5898240
  301.0 7.4 pad.14.clone
  308.4 6.0 reshape.97
  314.4 6.2 fusion.8
  320.6 5.2 fusion.9
  325.8 7.3 fusion.1
  336.1 3.3 reshape.121
  339.5 3.3 squeeze.162
  342.8 5.9 fusion.22
  348.7 4.3 squeeze.163
  353.0 4.2 squeeze.164
  357.2 4.7 squeeze.165
  361.9 4.3 squeeze.166
  379.2 3.3 squeeze.171
  382.5 11.6 %add_add_fusion.1 = f32[2,16,16,10,34]{4,3,2,1,0:T(8,128)} fusion(f32[2,16,16,10,34]{4,3,2,1,0:T(8,128)} %squeeze.165, f32[2,16,16,10,34]{4,3,2,1,0:T(8,128)} %squeeze.164, f32[2,16,16,10,34]{4,3,2,1,0:T(8,128)} %squeeze.163, f32[2,16,16,10,34]{4,3,2,1,0:T(8,128)} %reshape.121, f32[2,16,16,10,34]{4,3,2,1,0:T(8,128)} %squeeze.162), kind=kLoop, calls=%fused_computation.15 | loop fusion | flops 696320 | bytes 4177920 | tf_op jit(solution)/shard_map/add | solution.py:65
  394.2 7.8 fusion.11
  404.6 46.4 %collective-permute-done.8 = f32[2,16,16,8,32]{4,3,2,1,0:T(8,128)S(1)} collective-permute-done((f32[2,16,16,8,32]{4,3,2,1,0:T(8,128)}, f32[2,16,16,8,32]{4,3,2,1,0:T(8,128)S(1)}, u32[]{:S(2)}, u32[]{:S(2)}) %collective-permute-start.8) | collective-permute-done | bytes 524320 | tf_op jit(solution)/shard_map/ppermute | solution.py:22
  451.0 4.5 collective-permute-start.9
  455.5 90.5 %collective-permute-done.9 = f32[2,16,16,8,32]{4,3,2,1,0:T(8,128)S(1)} collective-permute-done((f32[2,16,16,8,32]{4,3,2,1,0:T(8,128)S(1)}, f32[2,16,16,8,32]{4,3,2,1,0:T(8,128)S(1)}, u32[]{:S(2)}, u32[]{:S(2)}) %collective-permute-start.9) | collective-permute-done | bytes 524320 | tf_op jit(solution)/shard_map/ppermute | solution.py:22
  546.0 4.3 collective-permute-done.10
  554.9 89.3 %collective-permute-done.11 = f32[2,16,16,8,32]{4,3,2,1,0:T(8,128)S(1)} collective-permute-done((f32[2,16,16,8,32]{4,3,2,1,0:T(8,128)S(1)}, f32[2,16,16,8,32]{4,3,2,1,0:T(8,128)S(1)}, u32[]{:S(2)}, u32[]{:S(2)}) %collective-permute-start.11) | collective-permute-done | bytes 524320 | tf_op jit(solution)/shard_map/ppermute | solution.py:13
  646.7 8.0 fusion.12
  659.4 8.4 %pad_maximum_fusion.1 = f32[2,64,16,8,32]{4,3,2,1,0:T(8,128)} fusion(f32[2,32,16,8,32]{4,3,2,1,0:T(8,128)} %maximum_select_fusion.1, f32[2,32,16,8,32]{4,3,2,1,0:T(8,128)} %all-gather.5.cloned.1.call-done), kind=kLoop, calls=%fused_computation.7 | loop fusion | flops 524288 | bytes 4194304 | tf_op jit(solution)/shard_map/concatenate | solution.py:90
  667.8 7.8 copy.21
  682.9 8.4 %copy.26 = f32[2,64,18,10,32]{1,0,4,3,2:T(2,128)} copy(f32[2,64,18,10,32]{1,4,3,2,0:T(8,128)S(1)} %pad_maximum_fusion.3) | data formatting | bytes 5898240
  691.3 7.4 pad.16.clone
  698.7 6.0 reshape.98
  704.8 6.2 fusion.6
  711.0 5.2 fusion.7
  716.2 7.5 fusion.4
  726.7 3.4 reshape.122
  733.4 5.9 fusion.20
  739.3 4.2 squeeze.185
  743.5 4.2 squeeze.186
  747.7 4.4 squeeze.187
  752.1 4.3 squeeze.188
  759.7 3.3 squeeze.190
  769.6 3.3 squeeze.193
  772.9 11.6 %add_add_fusion = f32[2,16,16,10,34]{4,3,2,1,0:T(8,128)} fusion(f32[2,16,16,10,34]{4,3,2,1,0:T(8,128)} %squeeze.187, f32[2,16,16,10,34]{4,3,2,1,0:T(8,128)} %squeeze.186, f32[2,16,16,10,34]{4,3,2,1,0:T(8,128)} %squeeze.185, f32[2,16,16,10,34]{4,3,2,1,0:T(8,128)} %reshape.122, f32[2,16,16,10,34]{4,3,2,1,0:T(8,128)} %squeeze.184), kind=kLoop, calls=%fused_computation.14 | loop fusion | flops 696320 | bytes 4177920 | tf_op jit(solution)/shard_map/add | solution.py:65
  784.5 7.8 fusion.10
  (79 shorter events, 79.0 us)
Async XLA Ops:
  6.5 250.7 %all-gather.3.cloned.1.call-start = ((), (), s32[]{:S(2)}) async-start(), calls=%async_computation | async-start | bytes 6291456 | tf_op jit(solution)/shard_map/all_gather | solution.py:87
  9.1 141.5 %copy-start.6 = (f32[2,16,16,8,32]{4,3,2,1,0:T(8,128)}, f32[2,16,16,8,32]{4,3,2,1,0:T(8,128)S(1)}, u32[]{:S(2)}) copy-start(f32[2,16,16,8,32]{4,3,2,1,0:T(8,128)S(1)} %broadcast_select_fusion) | copy-start | bytes 1572868
  9.2 148.8 %copy-start.10 = (f32[2]{0:T(128)S(1)}, f32[2]{0:T(128)}, u32[]{:S(2)}) copy-start(f32[2]{0:T(128)} %constant.14.clone) | copy-start | bytes 28
  9.2 48.7 %collective-permute-start = (f32[2,16,16,8,32]{4,3,2,1,0:T(8,128)S(1)}, f32[2,16,16,8,32]{4,3,2,1,0:T(8,128)S(1)}, u32[]{:S(2)}, u32[]{:S(2)}) collective-permute-start(f32[2,16,16,8,32]{4,3,2,1,0:T(8,128)S(1)} %broadcast_select_fusion), channel_id=1, source_target_pairs={{0,4},{4,0},{8,12},{12,8},{1,5},{5,1},{9,13},{13,9},{2,6},{6,2},{1... | collective-permute-start | bytes 1572872 | tf_op jit(solution)/shard_map/ppermute | solution.py:22
  57.9 92.7 %collective-permute-start.1 = (f32[2,16,16,8,32]{4,3,2,1,0:T(8,128)S(1)}, f32[2,16,16,8,32]{4,3,2,1,0:T(8,128)}, u32[]{:S(2)}, u32[]{:S(2)}) collective-permute-start(f32[2,16,16,8,32]{4,3,2,1,0:T(8,128)S(1)} %collective-permute-done), channel_id=1, source_target_pairs={{0,8},{4,12},{8,0},{12,4},{1,9},{5,13},{9,1},{13,5},{2,10},{6,14},... | collective-permute-start | bytes 1572872 | tf_op jit(solution)/shard_map/ppermute | solution.py:22
  150.7 4.5 collective-permute-start.2
  150.7 10.3 %copy-start.9 = (f32[27,2,16,64]{3,2,1,0:T(8,128)S(1)}, f32[27,2,16,64]{3,2,1,0:T(8,128)}, u32[]{:S(2)}) copy-start(f32[27,2,16,64]{3,2,1,0:T(8,128)} %param.6) | copy-start | bytes 663556
  150.7 496.0 %all-gather.5.cloned.1.call-start = ((), (), s32[]{:S(2)}) async-start(), calls=%async_computation.1 | async-start | bytes 6291456 | tf_op jit(solution)/shard_map/all_gather | solution.py:87
  159.6 92.6 %collective-permute-start.3 = (f32[2,16,16,8,32]{4,3,2,1,0:T(8,128)}, f32[2,16,16,8,32]{4,3,2,1,0:T(8,128)S(1)}, u32[]{:S(2)}, u32[]{:S(2)}) collective-permute-start(f32[2,16,16,8,32]{4,3,2,1,0:T(8,128)} %broadcast_multiply_fusion.1), channel_id=1, source_target_pairs={{0,2},{2,0},{1,3},{3,1},{4,6},{6,4},{5,7},{7,5},{8,10},{10,8},{9,1... | collective-permute-start | bytes 1572872 | tf_op jit(solution)/shard_map/ppermute | solution.py:13
  266.1 19.5 %collective-permute-start.4 = (f32[2,64,16,1,32]{1,4,3,2,0:T(8,128)S(1)}, f32[2,64,16,1,32]{1,4,3,2,0:T(8,128)S(1)}, u32[]{:S(2)}, u32[]{:S(2)}) collective-permute-start(f32[2,64,16,1,32]{1,4,3,2,0:T(8,128)S(1)} %copy.15), channel_id=1, source_target_pairs={{0,4},{4,8},{8,12},{1,5},{5,9},{9,13},{2,6},{6,10},{10,14},{3,7},{... | collective-permute-start | bytes 786440 | tf_op jit(solution)/shard_map/ppermute | solution.py:32
  268.2 17.5 %collective-permute-start.5 = (f32[2,64,16,1,32]{1,4,3,2,0:T(8,128)S(1)}, f32[2,64,16,1,32]{1,4,3,2,0:T(8,128)S(1)}, u32[]{:S(2)}, u32[]{:S(2)}) collective-permute-start(f32[2,64,16,1,32]{1,4,3,2,0:T(8,128)S(1)} %copy.16), channel_id=1, source_target_pairs={{4,0},{8,4},{12,8},{5,1},{9,5},{13,9},{6,2},{10,6},{14,10},{7,3},{... | collective-permute-start | bytes 786440 | tf_op jit(solution)/shard_map/ppermute | solution.py:33
  285.6 6.2 copy-start
  286.9 4.2 collective-permute-start.6
  288.3 3.5 collective-permute-start.7
  314.4 6.2 copy-start.7
  382.5 11.6 %copy-start.2 = (f32[2,16,16,8,32]{4,3,2,1,0:T(8,128)S(1)}, f32[2,16,16,8,32]{4,3,2,1,0:T(8,128)}, u32[]{:S(2)}) copy-start(f32[2,16,16,8,32]{4,3,2,1,0:T(8,128)} %param.4) | copy-start | bytes 1572868
  382.5 11.6 %copy-start.5 = (f32[2,16,16,10,34]{4,3,2,1,0:T(8,128)S(1)}, f32[2,16,16,10,34]{4,3,2,1,0:T(8,128)}, u32[]{:S(2)}) copy-start(f32[2,16,16,10,34]{4,3,2,1,0:T(8,128)} %squeeze.166) | copy-start | bytes 2088964
  401.9 49.0 %collective-permute-start.8 = (f32[2,16,16,8,32]{4,3,2,1,0:T(8,128)}, f32[2,16,16,8,32]{4,3,2,1,0:T(8,128)S(1)}, u32[]{:S(2)}, u32[]{:S(2)}) collective-permute-start(f32[2,16,16,8,32]{4,3,2,1,0:T(8,128)} %fusion.11), channel_id=1, source_target_pairs={{0,4},{4,0},{8,12},{12,8},{1,5},{5,1},{9,13},{13,9},{2,6},{6,2},{1... | collective-permute-start | bytes 1572872 | tf_op jit(solution)/shard_map/ppermute | solution.py:22
  451.0 95.1 %collective-permute-start.9 = (f32[2,16,16,8,32]{4,3,2,1,0:T(8,128)S(1)}, f32[2,16,16,8,32]{4,3,2,1,0:T(8,128)S(1)}, u32[]{:S(2)}, u32[]{:S(2)}) collective-permute-start(f32[2,16,16,8,32]{4,3,2,1,0:T(8,128)S(1)} %collective-permute-done.8), channel_id=1, source_target_pairs={{0,8},{4,12},{8,0},{12,4},{1,9},{5,13},{9,1},{13,5},{2,10},{6,14},... | collective-permute-start | bytes 1572872 | tf_op jit(solution)/shard_map/ppermute | solution.py:22
  546.0 4.3 collective-permute-start.10
  553.4 90.8 %collective-permute-start.11 = (f32[2,16,16,8,32]{4,3,2,1,0:T(8,128)S(1)}, f32[2,16,16,8,32]{4,3,2,1,0:T(8,128)S(1)}, u32[]{:S(2)}, u32[]{:S(2)}) collective-permute-start(f32[2,16,16,8,32]{4,3,2,1,0:T(8,128)S(1)} %broadcast_multiply_fusion), channel_id=1, source_target_pairs={{0,2},{2,0},{1,3},{3,1},{4,6},{6,4},{5,7},{7,5},{8,10},{10,8},{9,1... | collective-permute-start | bytes 1572872 | tf_op jit(solution)/shard_map/ppermute | solution.py:13
  655.3 20.4 %collective-permute-start.12 = (f32[2,64,16,1,32]{1,4,3,2,0:T(8,128)S(1)}, f32[2,64,16,1,32]{1,4,3,2,0:T(8,128)S(1)}, u32[]{:S(2)}, u32[]{:S(2)}) collective-permute-start(f32[2,64,16,1,32]{1,4,3,2,0:T(8,128)S(1)} %copy.19), channel_id=1, source_target_pairs={{0,4},{4,8},{8,12},{1,5},{5,9},{9,13},{2,6},{6,10},{10,14},{3,7},{... | collective-permute-start | bytes 786440 | tf_op jit(solution)/shard_map/ppermute | solution.py:32
  658.1 17.6 %collective-permute-start.13 = (f32[2,64,16,1,32]{1,4,3,2,0:T(8,128)S(1)}, f32[2,64,16,1,32]{1,4,3,2,0:T(8,128)S(1)}, u32[]{:S(2)}, u32[]{:S(2)}) collective-permute-start(f32[2,64,16,1,32]{1,4,3,2,0:T(8,128)S(1)} %copy.20), channel_id=1, source_target_pairs={{4,0},{8,4},{12,8},{5,1},{9,5},{13,9},{6,2},{10,6},{14,10},{7,3},{... | collective-permute-start | bytes 786440 | tf_op jit(solution)/shard_map/ppermute | solution.py:33
  675.7 6.5 copy-start.1
  676.9 3.0 collective-permute-start.14
  678.7 3.5 collective-permute-start.15
  704.8 6.2 copy-start.8
  772.9 11.6 %copy-start.3 = (f32[2,16,16,8,32]{4,3,2,1,0:T(8,128)S(1)}, f32[2,16,16,8,32]{4,3,2,1,0:T(8,128)}, u32[]{:S(2)}) copy-start(f32[2,16,16,8,32]{4,3,2,1,0:T(8,128)} %param.4) | copy-start | bytes 1572868
  772.9 11.6 %copy-start.4 = (f32[2,16,16,10,34]{4,3,2,1,0:T(8,128)S(1)}, f32[2,16,16,10,34]{4,3,2,1,0:T(8,128)}, u32[]{:S(2)}) copy-start(f32[2,16,16,10,34]{4,3,2,1,0:T(8,128)} %squeeze.188) | copy-start | bytes 2088964
Sparse Core Ops, SparseCore 0:
  150.8 101.8 all-gather.2
  546.2 100.0 all-gather.4
